TPU v7x, 32 devices: a whole 2x2x4 slice. The times are simulated.
32 devices in a mesh: brow: 4 (over y, x), bcol: 8 (over z, core).
Axes of the slice: x: 2, y: 2, z: 4, core: 2. Of those that a mesh axis runs over, the one named last changes fastest.
Arguments:
- gradient: bfloat16 [2048, 2048], P(('brow', 'bcol')), may hold values from -1.5 to 1.5
- left_stats: float32 [4, 2048, 512], P('brow', 'bcol'), may hold values from -1 to 8, as said below
- right_stats: float32 [4, 2048, 512], P('brow', 'bcol'), may hold values from -1 to 8, as said below
- left_roots: bfloat16 [4, 2048, 512], P('brow', 'bcol'), may hold values from -1 to 3, as said below
- right_roots: bfloat16 [4, 2048, 512], P('brow', 'bcol'), may hold values from -1 to 3, as said below
- refresh: int32 [4, 1], P('brow'), may hold values from 0 to 3, as said below
Outputs:
- update: bfloat16 [2048, 2048], P(('brow', 'bcol'))
- new_left_stats: float32 [4, 2048, 512], P('brow', 'bcol')
- new_right_stats: float32 [4, 2048, 512], P('brow', 'bcol')
- new_left_roots: bfloat16 [4, 2048, 512], P('brow', 'bcol')
- new_right_roots: bfloat16 [4, 2048, 512], P('brow', 'bcol')
Inputs may be any that keep to these rules, and one draw needn't show every extreme that they name: `refresh`: each row names 1 different block columns; some block row lists column 3 and another block row lists column 0. `left_stats`: every 512 x 512 block is symmetric positive definite. `right_stats`: every 512 x 512 block is symmetric positive definite. `left_roots`: every 512 x 512 block is symmetric. `right_roots`: every 512 x 512 block is symmetric.
All inputs are finite; a program needn't handle non-finite values.
Results may differ from a plain program's by a relative error of at most 0.005.
Values may be sent and summed in bfloat16 or wider, within the bound.
No kernel may reach another device: no remote copies, remote signals or barrier semaphores. Data moves between devices by JAX's collectives and lax.ppermute only.
A program may use at most 64 MiB of HBM per device.

v0:
```python
import jax
import jax.numpy as jnp
from jax import lax
from jax.sharding import PartitionSpec as P

ITERS = 3
decay = 0.9
epsilon = 1e-06
highest = lax.Precision.HIGHEST


def from_partner(shard, axis, stride):
    return lax.ppermute(shard, axis, [(i, i ^ 1 << stride) for i in range(lax.axis_size(axis))])


def product(left_side, right_side):
    return jnp.dot(left_side, right_side, precision=highest)


def unchanged(matrix):
    return matrix


def inverse_rows(row_block, collect):
    row_count, order_size = row_block.shape
    eye_rows = (
        lax.broadcasted_iota(jnp.int32, (row_count, order_size), 0)
        == lax.broadcasted_iota(jnp.int32, (row_count, order_size), 1)
    ).astype(jnp.float32)
    eye_full = jnp.eye(order_size, dtype=jnp.float32)
    shifted = row_block + epsilon * eye_rows
    whole_matrix = collect(shifted)
    scaling = 2.5 / jnp.sqrt(jnp.sum(whole_matrix * whole_matrix))
    moment_full = scaling * whole_matrix
    iterate = jnp.sqrt(jnp.sqrt(scaling)) * eye_rows
    for iteration in range(ITERS):
        factor = (5.0 * eye_full - moment_full) * 0.25
        square = product(factor, factor)
        fourth_rows = product(square, square)
        moment_rows = product(fourth_rows, moment_full)
        iterate = product(iterate, factor)
        if iteration + 1 < ITERS:
            moment_full = collect(moment_rows)
    return iterate.astype(jnp.bfloat16)


def body(gradient, left_stats, right_stats, left_roots, right_roots, refresh):
    position = lax.axis_index("bcol")
    half = position % 2
    block_col = position // 2
    order_size = left_stats.shape[2]
    half_rows = order_size // 2
    is_second = half == 1
    mine = lax.all_to_all(gradient, "bcol", split_axis=1, concat_axis=0, tiled=True)
    left_root_mine = left_roots[0]
    partner_grad, partner_left = from_partner((mine, left_root_mine), "bcol", 0)
    grad_full = jnp.where(
        is_second,
        jnp.concatenate([partner_grad, mine], 1),
        jnp.concatenate([mine, partner_grad], 1),
    )
    left_root_full = jnp.where(
        is_second,
        jnp.concatenate([partner_left, left_root_mine], 0),
        jnp.concatenate([left_root_mine, partner_left], 0),
    )
    grad_rows = lax.dynamic_slice_in_dim(grad_full, half * half_rows, half_rows, 0)
    left_gram = lax.dot_general(
        grad_rows, grad_full, (((1,), (1,)), ((), ())), preferred_element_type=jnp.float32
    )
    right_gram = lax.dot_general(
        mine, grad_full, (((0,), (0,)), ((), ())), preferred_element_type=jnp.float32
    )
    left_new = decay * left_stats[0] + (1.0 - decay) * left_gram
    right_new = decay * right_stats[0] + (1.0 - decay) * right_gram
    right_part = lax.dot_general(
        grad_full, right_roots[0], (((1,), (1,)), ((), ())), preferred_element_type=jnp.float32
    ).astype(jnp.bfloat16)
    update_cols = jnp.dot(left_root_full, right_part, preferred_element_type=jnp.float32).astype(
        jnp.bfloat16
    )
    update = lax.all_to_all(update_cols, "bcol", split_axis=0, concat_axis=1, tiled=True)
    chosen = refresh[0]
    listed = jnp.any(chosen == block_col)
    mine_side = jnp.where(is_second, right_new, left_new)
    partner_side = from_partner(
        jnp.where(is_second, left_new, right_new).astype(jnp.bfloat16), "bcol", 0
    ).astype(jnp.float32)
    whole_side = jnp.where(
        is_second,
        jnp.concatenate([partner_side, mine_side], 0),
        jnp.concatenate([mine_side, partner_side], 0),
    )
    root_full = inverse_rows(whole_side, unchanged)
    own_rows = lax.dynamic_slice_in_dim(root_full, half * half_rows, half_rows, 0)
    given_rows = lax.dynamic_slice_in_dim(root_full, (1 - half) * half_rows, half_rows, 0)
    taken = from_partner(given_rows, "bcol", 0)
    left_fresh = jnp.where(is_second, taken, own_rows)
    right_fresh = jnp.where(is_second, own_rows, taken)
    left_out = jnp.where(listed, left_fresh, left_roots[0])
    right_out = jnp.where(listed, right_fresh, right_roots[0])
    return (update, left_new[None], right_new[None], left_out[None], right_out[None])


def solution(mesh):
    in_specs = (
        P(("brow", "bcol"), None),
        P("brow", "bcol", None),
        P("brow", "bcol", None),
        P("brow", "bcol", None),
        P("brow", "bcol", None),
        P("brow", None),
    )
    out_specs = (
        P(("brow", "bcol"), None),
        P("brow", "bcol", None),
        P("brow", "bcol", None),
        P("brow", "bcol", None),
        P("brow", "bcol", None),
    )
    return jax.shard_map(body, mesh=mesh, in_specs=in_specs, out_specs=out_specs, check_vma=False)
```

profile of v0, /device:TPU:0, one launch (start us, length us, event | category | flops | bytes accessed | tf_op | source)
XLA Modules:
  0.0 51.4 jit_solution(1072921021482301779)
XLA Ops:
  0.6 1.7 %copy.16 = bf16[8,8,8,256]{3,2,0,1:T(8,128)(2,1)} copy(bf16[8,8,8,256]{3,2,1,0:T(8,128)(2,1)} %bitcast.59) | data formatting | bytes 524288 | tf_op jit(solution)/shard_map/all_to_all | solution.py:54
  2.3 0.0 copy-start.3
  2.3 0.0 copy-start.5
  2.3 6.5 %all-to-all-start = ((bf16[64,8,256]{2,0,1:T(8,128)(2,1)}), bf16[64,8,256]{2,0,1:T(8,128)(2,1)S(1)}, u32[]{:S(2)}, u32[]{:S(2)}) async-start(bf16[64,8,256]{2,0,1:T(8,128)(2,1)} %bitcast.48), calls=%async_computation | async-start | bytes 524288 | tf_op jit(solution)/shard_map/all_to_all | solution.py:54
  8.8 0.0 copy-done.3
  8.8 0.5 collective-permute-start
  9.3 9.2 %all-to-all-done = bf16[64,8,256]{2,0,1:T(8,128)(2,1)S(1)} async-done(((bf16[64,8,256]{2,0,1:T(8,128)(2,1)}), bf16[64,8,256]{2,0,1:T(8,128)(2,1)S(1)}, u32[]{:S(2)}, u32[]{:S(2)}) %all-to-all-start) | async-done | bytes 262176 | tf_op jit(solution)/shard_map/all_to_all | solution.py:54
  18.5 0.0 collective-permute-start.1
  18.5 0.0 collective-permute-done
  18.5 1.5 %collective-permute-done.1 = bf16[512,256]{1,0:T(8,128)(2,1)S(1)} collective-permute-done((bf16[512,256]{1,0:T(8,128)(2,1)S(1)}, bf16[512,256]{1,0:T(8,128)(2,1)S(1)}, u32[]{:S(2)}, u32[]{:S(2)}) %collective-permute-start.1) | collective-permute-done | bytes 262176 | tf_op jit(solution)/shard_map/ppermute | solution.py:13
  20.0 0.0 copy-done.5
  20.0 1.5 %convolution_convert_fusion.1 = bf16[512,256]{1,0:T(8,128)(2,1)} fusion(bf16[256,512]{1,0:T(8,128)(2,1)S(1)} %bitcast.58, bf16[256,512]{1,0:T(8,128)(2,1)S(1)} %collective-permute-done, pred[]{:T(512)S(6)} %eq.23, bf16[1,256,512]{2,1,0:T(8,128)(2,1)S(1)} %copy-done.5, bf16[512,256]{1,0:T(8,128)(2,1)S(1)} %bitcast.54, ...), kind=kOutput, calls=%fused_computation.10 | convolution fusion | flops 273416192 | bytes 1572865 | tf_op jit(solution)/shard_map/dot_general | solution.py:79
  21.5 3.4 %all-to-all-start.1 = ((bf16[8,64,256]{2,1,0:T(8,128)(2,1)}), bf16[8,64,256]{2,1,0:T(8,128)(2,1)S(1)}, u32[]{:S(2)}, u32[]{:S(2)}) async-start(bf16[8,64,256]{2,1,0:T(8,128)(2,1)} %bitcast.5), calls=%async_computation.1 | async-start | bytes 524288 | tf_op jit(solution)/shard_map/all_to_all | solution.py:82
  24.9 0.0 copy-start.7
  25.0 0.1 maximum_select_fusion.3
  25.1 0.9 %copy-done.7 = f32[1,256,512]{2,1,0:T(8,128)S(1)} copy-done((f32[1,256,512]{2,1,0:T(8,128)S(1)}, f32[1,256,512]{2,1,0:T(8,128)}, u32[]{:S(2)}) %copy-start.7) | copy-done | bytes 524312
  26.0 0.0 copy-start.2
  26.0 0.3 fusion.2
  26.3 0.7 %copy-done.2 = f32[1,256,512]{2,1,0:T(8,128)S(1)} copy-done((f32[1,256,512]{2,1,0:T(8,128)S(1)}, f32[1,256,512]{2,1,0:T(8,128)}, u32[]{:S(2)}) %copy-start.2) | copy-done | bytes 524312
  27.0 0.0 copy-start
  27.0 0.4 select_convert_fusion
  27.4 0.0 copy-start.1
  27.4 0.5 collective-permute-start.2
  27.9 0.0 copy-done
  27.9 0.1 broadcast_select_fusion
  28.0 0.2 copy-done.1
  28.2 0.8 %collective-permute-done.2 = bf16[256,512]{1,0:T(8,128)(2,1)S(1)} collective-permute-done((bf16[256,512]{1,0:T(8,128)(2,1)S(1)}, bf16[256,512]{1,0:T(8,128)(2,1)S(1)}, u32[]{:S(2)}, u32[]{:S(2)}) %collective-permute-start.2) | collective-permute-done | bytes 262176 | tf_op jit(solution)/shard_map/ppermute | solution.py:13
  29.1 0.9 %multiply_reduce_fusion = f32[]{:T(128)} fusion(f32[256,512]{1,0:T(8,128)S(1)} %convert_element_type.20, f32[256,512]{1,0:T(8,128)S(1)} %broadcast_select_fusion, pred[]{:T(512)S(6)} %eq.23), kind=kLoop, calls=%fused_computation.18 | loop fusion | flops 2097151 | bytes 1048581 | tf_op jit(solution)/shard_map/reduce_sum | solution.py:33
  30.7 2.1 %fusion.15 = f32[512,512]{1,0:T(8,128)S(1)} fusion(f32[]{:T(128)S(6)} %div.14, f32[256,512]{1,0:T(8,128)S(1)} %broadcast_select_fusion, f32[256,512]{1,0:T(8,128)S(1)} %convert_element_type.20, pred[]{:T(512)S(6)} %eq.23), kind=kOutput, calls=%fused_computation.24 | convolution fusion | flops 1613234176 | bytes 2097157 | tf_op jit(solution)/shard_map/dot_general | solution.py:17
  32.8 1.9 %fusion.7 = f32[512,512]{1,0:T(8,128)S(1)} fusion(f32[]{:T(128)S(6)} %div.14, f32[]{:T(128)S(6)} %sqrt.11, f32[256,512]{1,0:T(8,128)S(1)} %broadcast_select_fusion, f32[256,512]{1,0:T(8,128)S(1)} %convert_element_type.20, pred[]{:T(512)S(6)} %eq.23), kind=kOutput, calls=%fused_computation.16 | convolution fusion | flops 1613758464 | bytes 2097161 | tf_op jit(solution)/shard_map/dot_general | solution.py:17
  34.8 1.8 %fusion.61 = f32[512,512]{1,0:T(8,128)S(1)} fusion(f32[512,512]{1,0:T(8,128)S(1)} %fusion.15), kind=kOutput, calls=%fused_computation.72 | convolution fusion | flops 1610612736 | bytes 2097152 | tf_op jit(solution)/shard_map/dot_general | solution.py:17
  36.6 1.9 %fusion.9 = f32[512,512]{1,0:T(8,128)S(1)} fusion(f32[512,512]{1,0:T(8,128)S(1)} %fusion.61, f32[]{:T(128)S(6)} %div.14, f32[256,512]{1,0:T(8,128)S(1)} %broadcast_select_fusion, f32[256,512]{1,0:T(8,128)S(1)} %convert_element_type.20, pred[]{:T(512)S(6)} %eq.23), kind=kOutput, calls=%fused_computation.20 | convolution fusion | flops 1612447744 | bytes 3145733 | tf_op jit(solution)/shard_map/dot_general | solution.py:17
  38.6 1.9 %fusion.11 = f32[512,512]{1,0:T(8,128)S(1)} fusion(f32[512,512]{1,0:T(8,128)S(1)} %fusion.9), kind=kOutput, calls=%fused_computation.22 | convolution fusion | flops 1611661312 | bytes 2097152 | tf_op jit(solution)/shard_map/dot_general | solution.py:17
  40.5 1.9 %fusion.13 = f32[512,512]{1,0:T(8,128)S(1)} fusion(f32[512,512]{1,0:T(8,128)S(1)} %fusion.7, f32[512,512]{1,0:T(8,128)S(1)} %fusion.9), kind=kOutput, calls=%fused_computation.23 | convolution fusion | flops 1611661312 | bytes 3145728 | tf_op jit(solution)/shard_map/dot_general | solution.py:17
  42.4 2.0 %fusion.62 = f32[512,512]{1,0:T(8,128)S(1)} fusion(f32[512,512]{1,0:T(8,128)S(1)} %fusion.11), kind=kOutput, calls=%fused_computation.73 | convolution fusion | flops 1610612736 | bytes 2097152 | tf_op jit(solution)/shard_map/dot_general | solution.py:17
  44.5 1.9 %fusion = f32[512,512]{1,0:T(8,128)S(1)} fusion(f32[512,512]{1,0:T(8,128)S(1)} %fusion.62, f32[512,512]{1,0:T(8,128)S(1)} %fusion.9), kind=kOutput, calls=%fused_computation.3 | convolution fusion | flops 1611661312 | bytes 3145728 | tf_op jit(solution)/shard_map/dot_general | solution.py:17
  46.3 1.9 %convolution_convert_fusion = bf16[512,512]{1,0:T(8,128)(2,1)S(1)} fusion(f32[512,512]{1,0:T(8,128)S(1)} %fusion.13, f32[512,512]{1,0:T(8,128)S(1)} %fusion), kind=kOutput, calls=%fused_computation.4 | convolution fusion | flops 1610874880 | bytes 2621440 | tf_op jit(solution)/shard_map/dot_general | solution.py:17
  48.2 0.4 collective-permute-start.3
  49.3 0.0 all-to-all-done.1
  49.4 0.0 copy-start.4
  49.4 0.0 copy-start.6
  49.4 0.7 %copy.14 = bf16[8,8,8,256]{3,2,0,1:T(8,128)(2,1)} copy(bf16[8,8,8,256]{3,2,1,0:T(8,128)(2,1)S(1)} %bitcast.52) | data formatting | bytes 524288 | tf_op jit(solution)/shard_map/all_to_all | solution.py:82
  50.1 0.0 collective-permute-done.3
  50.1 0.3 copy-done.4
  50.4 0.1 copy-done.6
  50.5 0.9 %fusion.42 = (bf16[1,256,512]{2,1,0:T(8,128)(2,1)}, bf16[1,256,512]{2,1,0:T(8,128)(2,1)}) fusion(bf16[1,256,512]{2,1,0:T(8,128)(2,1)S(1)} %copy-done.6, bf16[256,512]{1,0:T(8,128)(2,1)S(1)} %collective-permute-done.3, pred[]{:T(512)S(6)} %eq.23, pred[]{:T(512)} %bitcast.14, bf16[512,512]{1,0:T(8,128)(2,1)S(1)} %convolution_convert_fusion, s32[]{:T(128)S(6)} %select_n.72, ...), kind=kLoop, calls=%fused_computation.53 | loop fusion | flops 524288 | bytes 1572870 | tf_op jit(solution)/shard_map/broadcast_in_dim | solution.py:102
  (2 shorter events, 0.1 us)
Async XLA Ops:
  2.3 6.5 %copy-start.3 = (bf16[1,256,512]{2,1,0:T(8,128)(2,1)S(1)}, bf16[1,256,512]{2,1,0:T(8,128)(2,1)}, u32[]{:S(2)}) copy-start(bf16[1,256,512]{2,1,0:T(8,128)(2,1)} %param.9) | copy-start | bytes 786436
  2.3 17.7 %copy-start.5 = (bf16[1,256,512]{2,1,0:T(8,128)(2,1)S(1)}, bf16[1,256,512]{2,1,0:T(8,128)(2,1)}, u32[]{:S(2)}) copy-start(bf16[1,256,512]{2,1,0:T(8,128)(2,1)} %param.10) | copy-start | bytes 786436
  2.3 16.2 %all-to-all-start = ((bf16[64,8,256]{2,0,1:T(8,128)(2,1)}), bf16[64,8,256]{2,0,1:T(8,128)(2,1)S(1)}, u32[]{:S(2)}, u32[]{:S(2)}) async-start(bf16[64,8,256]{2,0,1:T(8,128)(2,1)} %bitcast.48), calls=%async_computation | async-start | bytes 524288 | tf_op jit(solution)/shard_map/all_to_all | solution.py:54
  8.8 9.7 %collective-permute-start = (bf16[256,512]{1,0:T(8,128)(2,1)S(1)}, bf16[256,512]{1,0:T(8,128)(2,1)S(1)}, u32[]{:S(2)}, u32[]{:S(2)}) collective-permute-start(bf16[256,512]{1,0:T(8,128)(2,1)S(1)} %bitcast.57), channel_id=1, source_target_pairs={{0,1},{1,0},{2,3},{3,2},{4,5},{5,4},{6,7},{7,6},{8,9},{9,8},{10,11... | collective-permute-start | bytes 786440 | tf_op jit(solution)/shard_map/ppermute | solution.py:13
  18.5 1.5 %collective-permute-start.1 = (bf16[512,256]{1,0:T(8,128)(2,1)S(1)}, bf16[512,256]{1,0:T(8,128)(2,1)S(1)}, u32[]{:S(2)}, u32[]{:S(2)}) collective-permute-start(bf16[512,256]{1,0:T(8,128)(2,1)S(1)} %bitcast.53), channel_id=1, source_target_pairs={{0,1},{1,0},{2,3},{3,2},{4,5},{5,4},{6,7},{7,6},{8,9},{9,8},{10,11... | collective-permute-start | bytes 786440 | tf_op jit(solution)/shard_map/ppermute | solution.py:13
  21.5 27.8 %all-to-all-start.1 = ((bf16[8,64,256]{2,1,0:T(8,128)(2,1)}), bf16[8,64,256]{2,1,0:T(8,128)(2,1)S(1)}, u32[]{:S(2)}, u32[]{:S(2)}) async-start(bf16[8,64,256]{2,1,0:T(8,128)(2,1)} %bitcast.5), calls=%async_computation.1 | async-start | bytes 524288 | tf_op jit(solution)/shard_map/all_to_all | solution.py:82
  24.9 1.0 %copy-start.7 = (f32[1,256,512]{2,1,0:T(8,128)S(1)}, f32[1,256,512]{2,1,0:T(8,128)}, u32[]{:S(2)}) copy-start(f32[1,256,512]{2,1,0:T(8,128)} %param.8) | copy-start | bytes 1572868
  26.0 1.0 %copy-start.2 = (f32[1,256,512]{2,1,0:T(8,128)S(1)}, f32[1,256,512]{2,1,0:T(8,128)}, u32[]{:S(2)}) copy-start(f32[1,256,512]{2,1,0:T(8,128)} %param.7) | copy-start | bytes 1572868
  27.0 0.8 %copy-start = (f32[256,512]{1,0:T(8,128)}, f32[256,512]{1,0:T(8,128)S(1)}, u32[]{:S(2)}) copy-start(f32[256,512]{1,0:T(8,128)S(1)} %fusion.2) | copy-start | bytes 1572868
  27.4 0.8 %copy-start.1 = (f32[256,512]{1,0:T(8,128)}, f32[256,512]{1,0:T(8,128)S(1)}, u32[]{:S(2)}) copy-start(f32[256,512]{1,0:T(8,128)S(1)} %get-tuple-element.8) | copy-start | bytes 1572868
  27.4 1.6 %collective-permute-start.2 = (bf16[256,512]{1,0:T(8,128)(2,1)S(1)}, bf16[256,512]{1,0:T(8,128)(2,1)S(1)}, u32[]{:S(2)}, u32[]{:S(2)}) collective-permute-start(bf16[256,512]{1,0:T(8,128)(2,1)S(1)} %get-tuple-element.7), channel_id=1, source_target_pairs={{0,1},{1,0},{2,3},{3,2},{4,5},{5,4},{6,7},{7,6},{8,9},{9,8},{10,11... | collective-permute-start | bytes 786440 | tf_op jit(solution)/shard_map/ppermute | solution.py:13
  48.2 1.9 %collective-permute-start.3 = (bf16[256,512]{1,0:T(8,128)(2,1)S(1)}, bf16[256,512]{1,0:T(8,128)(2,1)S(1)}, u32[]{:S(2)}, u32[]{:S(2)}) collective-permute-start(bf16[256,512]{1,0:T(8,128)(2,1)S(1)} %constant_dynamic-slice_fusion), channel_id=1, source_target_pairs={{0,1},{1,0},{2,3},{3,2},{4,5},{5,4},{6,7},{7,6},{8,9},{9,8},{10,11... | collective-permute-start | bytes 786440 | tf_op jit(solution)/shard_map/ppermute | solution.py:13
  49.4 1.0 %copy-start.4 = (bf16[1,256,512]{2,1,0:T(8,128)(2,1)S(1)}, bf16[1,256,512]{2,1,0:T(8,128)(2,1)}, u32[]{:S(2)}) copy-start(bf16[1,256,512]{2,1,0:T(8,128)(2,1)} %param.9) | copy-start | bytes 786436
  49.4 1.1 %copy-start.6 = (bf16[1,256,512]{2,1,0:T(8,128)(2,1)S(1)}, bf16[1,256,512]{2,1,0:T(8,128)(2,1)}, u32[]{:S(2)}) copy-start(bf16[1,256,512]{2,1,0:T(8,128)(2,1)} %param.10) | copy-start | bytes 786436
where the time goes:
time: 51.9 us; the launch traced here: 51.4 us
  matrix products  19.5 us (38%)
  waiting for transfers between devices  11.6 us (22%)
  starting transfers between devices  11.3 us (22%)
  local copies, waits for them, and re-layouts  4.65 us (9%)
  between operations  2.24 us (4%)
  other arithmetic  2.1 us (4%)
    dot_general x9, matrix products, product(): return jnp.dot(left_side, right_side, precision=highest)  17.4 us
    all_to_all x1, waiting for transfers between devices, body(): lax.all_to_all(gradient, 'bcol', split_axis=1, concat_axis=0, tiled=True)  9.2 us
    all_to_all x1, starting transfers between devices, body(): lax.all_to_all(gradient, 'bcol', split_axis=1, concat_axis=0, tiled=True)  6.49 us
    all_to_all x1, starting transfers between devices, body(): lax.all_to_all(update_cols, 'bcol', split_axis=0, concat_axis=1, tiled=True)  3.41 us
    ppermute x4, waiting for transfers between devices, from_partner(): lax.ppermute(shard, axis, [(i, i ^ 1 << stride) for i in range(lax.axis_s...  2.38 us
    unnamed x16, local copies, waits for them, and re-layouts  2.23 us
    all_to_all x1, local copies, waits for them, and re-layouts, body(): lax.all_to_all(gradient, 'bcol', split_axis=1, concat_axis=0, tiled=True)  1.67 us
    dot_general x1, matrix products, body(): jnp.dot(left_root_full, right_part, preferred_element_type=jnp.float32)  1.48 us
  transfers between devices with their start and end apart: 6, of which 3 were waited for; matrix products, arithmetic and copies ran while one was open for 39% of the time, Pallas kernels for 0%

commit v1 on v0

--- a/solution.py
+++ b/solution.py
@@ -79,7 +79,12 @@
     update_cols = jnp.dot(left_root_full, right_part, preferred_element_type=jnp.float32).astype(
         jnp.bfloat16
     )
-    update = lax.all_to_all(update_cols, "bcol", split_axis=0, concat_axis=1, tiled=True)
+    update = jnp.concatenate(
+        lax.all_to_all(
+            jnp.stack(jnp.split(update_cols, lax.axis_size("bcol"), axis=0)), "bcol", 0, 0
+        ),
+        axis=1,
+    )
     chosen = refresh[0]
     listed = jnp.any(chosen == block_col)
     mine_side = jnp.where(is_second, right_new, left_new)

time: 51.9 us -> 56.2 us (1.083)
  local copies, waits for them, and re-layouts: 4.65 us -> 9.58 us
  matrix products: 19.5 us -> 18.8 us
    unnamed x16 -> x23, local copies, waits for them, and re-layouts: 2.23 us -> 6.55 us
    all_to_all x1 -> x0, local copies, waits for them, and re-layouts: 0.72 us -> none  [body(): lax.all_to_all(update_cols, 'bcol', split_axis=0, concat_axis=1, tiled=True)]
    reshape x0 -> x1, local copies, waits for them, and re-layouts: none -> 0.72 us  [body(): jnp.concatenate(lax.all_to_all(jnp.stack(jnp.split(update_cols, lax.axis_...]
    dot_general x1, matrix products: 1.48 us -> 0.77 us  [body(): jnp.dot(left_root_full, right_part, preferred_element_type=jnp.float32)]
    another operation x0 -> x1, local copies, waits for them, and re-layouts: none -> 0.62 us  [body(): jnp.stack(jnp.split(update_cols, lax.axis_size('bcol'), axis=0))]
  transfers between devices with their start and end apart: 6 -> 6, of which waited for: 3 -> 3; matrix products, arithmetic and copies ran while one was open for 39% -> 36% of each run, Pallas kernels for 0% -> 0%
where the time goes in v1:
time: 56.2 us; the launch traced here: 55.7 us
  matrix products  18.8 us (33%)
  waiting for transfers between devices  11.6 us (21%)
  starting transfers between devices  11.3 us (20%)
  local copies, waits for them, and re-layouts  9.58 us (17%)
  between operations  2.25 us (4%)
  other arithmetic  2.1 us (4%)
    dot_general x9, matrix products, product(): return jnp.dot(left_side, right_side, precision=highest)  17.4 us
    all_to_all x1, waiting for transfers between devices, body(): lax.all_to_all(gradient, 'bcol', split_axis=1, concat_axis=0, tiled=True)  9.2 us
    unnamed x23, local copies, waits for them, and re-layouts  6.55 us
    all_to_all x1, starting transfers between devices, body(): lax.all_to_all(gradient, 'bcol', split_axis=1, concat_axis=0, tiled=True)  6.49 us
    all_to_all x1, starting transfers between devices, body(): lax.all_to_all(jnp.stack(jnp.split(update_cols, lax.axis_size('bcol'), ax...  3.41 us
    ppermute x4, waiting for transfers between devices, from_partner(): lax.ppermute(shard, axis, [(i, i ^ 1 << stride) for i in range(lax.axis_s...  2.38 us
    all_to_all x1, local copies, waits for them, and re-layouts, body(): lax.all_to_all(gradient, 'bcol', split_axis=1, concat_axis=0, tiled=True)  1.67 us
    ppermute x4, starting transfers between devices, from_partner(): lax.ppermute(shard, axis, [(i, i ^ 1 << stride) for i in range(lax.axis_s...  1.4 us
  transfers between devices with their start and end apart: 6, of which 3 were waited for; matrix products, arithmetic and copies ran while one was open for 36% of the time, Pallas kernels for 0%

profile of v1, /device:TPU:0, one launch (start us, length us, event | category | flops | bytes accessed | tf_op | source)
XLA Modules:
  0.0 55.7 jit_solution(8330460665176747677)
XLA Ops:
  0.6 1.7 %copy.17 = bf16[8,8,8,256]{3,2,0,1:T(8,128)(2,1)} copy(bf16[8,8,8,256]{3,2,1,0:T(8,128)(2,1)} %bitcast.90) | data formatting | bytes 524288 | tf_op jit(solution)/shard_map/all_to_all | solution.py:54
  2.3 6.5 %all-to-all-start = ((bf16[64,8,256]{2,0,1:T(8,128)(2,1)}), bf16[64,8,256]{2,0,1:T(8,128)(2,1)S(1)}, u32[]{:S(2)}, u32[]{:S(2)}) async-start(bf16[64,8,256]{2,0,1:T(8,128)(2,1)} %bitcast.79), calls=%async_computation | async-start | bytes 524288 | tf_op jit(solution)/shard_map/all_to_all | solution.py:54
  8.8 0.0 copy-done.3
  8.8 0.5 collective-permute-start
  9.3 9.2 %all-to-all-done = bf16[64,8,256]{2,0,1:T(8,128)(2,1)S(1)} async-done(((bf16[64,8,256]{2,0,1:T(8,128)(2,1)}), bf16[64,8,256]{2,0,1:T(8,128)(2,1)S(1)}, u32[]{:S(2)}, u32[]{:S(2)}) %all-to-all-start) | async-done | bytes 262176 | tf_op jit(solution)/shard_map/all_to_all | solution.py:54
  18.5 0.0 collective-permute-start.1
  18.5 0.0 collective-permute-done
  18.5 1.5 %collective-permute-done.1 = bf16[512,256]{1,0:T(8,128)(2,1)S(1)} collective-permute-done((bf16[512,256]{1,0:T(8,128)(2,1)S(1)}, bf16[512,256]{1,0:T(8,128)(2,1)S(1)}, u32[]{:S(2)}, u32[]{:S(2)}) %collective-permute-start.1) | collective-permute-done | bytes 262176 | tf_op jit(solution)/shard_map/ppermute | solution.py:13
  20.0 0.8 %convolution_convert_fusion.1 = bf16[512,256]{1,0:T(8,128)(2,1)S(1)} fusion(bf16[256,512]{1,0:T(8,128)(2,1)S(1)} %bitcast.89, bf16[256,512]{1,0:T(8,128)(2,1)S(1)} %collective-permute-done, pred[]{:T(512)S(6)} %eq.23, bf16[1,256,512]{2,1,0:T(8,128)(2,1)S(1)} %copy-done.5, bf16[512,256]{1,0:T(8,128)(2,1)S(1)} %bitcast.85, ...), kind=kOutput, calls=%fused_computation.10 | convolution fusion | flops 273416192 | bytes 1572865 | tf_op jit(solution)/shard_map/dot_general | solution.py:79
  20.8 0.6 %fusion.51 = bf16[8,64,256]{2,1,0:T(8,128)(2,1)} fusion(bf16[512,256]{1,0:T(8,128)(2,1)S(1)} %convolution_convert_fusion.1), kind=kLoop, calls=%fused_computation.72 | loop fusion | bytes 65536
  21.4 0.6 %fusion.50 = bf16[8,64,256]{2,1,0:T(8,128)(2,1)} fusion(bf16[8,64,256]{2,1,0:T(8,128)(2,1)} %fusion.51, bf16[512,256]{1,0:T(8,128)(2,1)S(1)} %convolution_convert_fusion.1), kind=kLoop, calls=%fused_computation.70 | loop fusion | bytes 65536
  22.1 0.6 %fusion.49 = bf16[8,64,256]{2,1,0:T(8,128)(2,1)} fusion(bf16[8,64,256]{2,1,0:T(8,128)(2,1)} %fusion.50, bf16[512,256]{1,0:T(8,128)(2,1)S(1)} %convolution_convert_fusion.1), kind=kLoop, calls=%fused_computation.68 | loop fusion | bytes 65536
  22.7 0.6 %fusion.48 = bf16[8,64,256]{2,1,0:T(8,128)(2,1)} fusion(bf16[8,64,256]{2,1,0:T(8,128)(2,1)} %fusion.49, bf16[512,256]{1,0:T(8,128)(2,1)S(1)} %convolution_convert_fusion.1), kind=kLoop, calls=%fused_computation.66 | loop fusion | bytes 65536
  23.3 0.6 %fusion.47 = bf16[8,64,256]{2,1,0:T(8,128)(2,1)} fusion(bf16[8,64,256]{2,1,0:T(8,128)(2,1)} %fusion.48, bf16[512,256]{1,0:T(8,128)(2,1)S(1)} %convolution_convert_fusion.1), kind=kLoop, calls=%fused_computation.64 | loop fusion | bytes 65536
  23.9 0.6 %fusion.46 = bf16[8,64,256]{2,1,0:T(8,128)(2,1)} fusion(bf16[8,64,256]{2,1,0:T(8,128)(2,1)} %fusion.47, bf16[512,256]{1,0:T(8,128)(2,1)S(1)} %convolution_convert_fusion.1), kind=kLoop, calls=%fused_computation.62 | loop fusion | bytes 65536
  24.5 0.6 %fusion.45 = bf16[8,64,256]{2,1,0:T(8,128)(2,1)} fusion(bf16[8,64,256]{2,1,0:T(8,128)(2,1)} %fusion.46, bf16[512,256]{1,0:T(8,128)(2,1)S(1)} %convolution_convert_fusion.1), kind=kLoop, calls=%fused_computation.60 | loop fusion | bytes 65536
  25.1 0.6 %fusion.44 = bf16[8,64,256]{2,1,0:T(8,128)(2,1)} fusion(bf16[8,64,256]{2,1,0:T(8,128)(2,1)} %fusion.45, bf16[512,256]{1,0:T(8,128)(2,1)S(1)} %convolution_convert_fusion.1), kind=kLoop, calls=%fused_computation.58 | loop fusion | bytes 65536 | tf_op jit(solution)/shard_map/stack | solution.py:84
  25.8 3.4 %all-to-all-start.1 = ((bf16[8,64,256]{2,1,0:T(8,128)(2,1)}), bf16[8,64,256]{2,1,0:T(8,128)(2,1)S(1)}, u32[]{:S(2)}, u32[]{:S(2)}) async-start(bf16[8,64,256]{2,1,0:T(8,128)(2,1)} %fusion.44), calls=%async_computation.1 | async-start | bytes 524288 | tf_op jit(solution)/shard_map/all_to_all | solution.py:83
  29.2 0.0 copy-start.7
  29.2 0.1 maximum_select_fusion.3
  29.3 0.9 %copy-done.7 = f32[1,256,512]{2,1,0:T(8,128)S(1)} copy-done((f32[1,256,512]{2,1,0:T(8,128)S(1)}, f32[1,256,512]{2,1,0:T(8,128)}, u32[]{:S(2)}) %copy-start.7) | copy-done | bytes 524312
  30.2 0.3 fusion.2
  30.6 0.7 %copy-done.2 = f32[1,256,512]{2,1,0:T(8,128)S(1)} copy-done((f32[1,256,512]{2,1,0:T(8,128)S(1)}, f32[1,256,512]{2,1,0:T(8,128)}, u32[]{:S(2)}) %copy-start.2) | copy-done | bytes 524312
  31.3 0.4 select_convert_fusion
  31.6 0.0 copy-start.1
  31.6 0.5 collective-permute-start.2
  32.1 0.1 broadcast_select_fusion
  32.2 0.2 copy-done.1
  32.4 0.8 %collective-permute-done.2 = bf16[256,512]{1,0:T(8,128)(2,1)S(1)} collective-permute-done((bf16[256,512]{1,0:T(8,128)(2,1)S(1)}, bf16[256,512]{1,0:T(8,128)(2,1)S(1)}, u32[]{:S(2)}, u32[]{:S(2)}) %collective-permute-start.2) | collective-permute-done | bytes 262176 | tf_op jit(solution)/shard_map/ppermute | solution.py:13
  33.3 0.9 %multiply_reduce_fusion = f32[]{:T(128)} fusion(f32[256,512]{1,0:T(8,128)S(1)} %convert_element_type.20, f32[256,512]{1,0:T(8,128)S(1)} %broadcast_select_fusion, pred[]{:T(512)S(6)} %eq.23), kind=kLoop, calls=%fused_computation.18 | loop fusion | flops 2097151 | bytes 1048581 | tf_op jit(solution)/shard_map/reduce_sum | solution.py:33
  35.0 2.1 %fusion.15 = f32[512,512]{1,0:T(8,128)S(1)} fusion(f32[]{:T(128)S(6)} %div.14, f32[256,512]{1,0:T(8,128)S(1)} %broadcast_select_fusion, f32[256,512]{1,0:T(8,128)S(1)} %convert_element_type.20, pred[]{:T(512)S(6)} %eq.23), kind=kOutput, calls=%fused_computation.24 | convolution fusion | flops 1613234176 | bytes 2097157 | tf_op jit(solution)/shard_map/dot_general | solution.py:17
  37.1 1.9 %fusion.7 = f32[512,512]{1,0:T(8,128)S(1)} fusion(f32[]{:T(128)S(6)} %div.14, f32[]{:T(128)S(6)} %sqrt.11, f32[256,512]{1,0:T(8,128)S(1)} %broadcast_select_fusion, f32[256,512]{1,0:T(8,128)S(1)} %convert_element_type.20, pred[]{:T(512)S(6)} %eq.23), kind=kOutput, calls=%fused_computation.16 | convolution fusion | flops 1613758464 | bytes 2097161 | tf_op jit(solution)/shard_map/dot_general | solution.py:17
  39.0 1.8 %fusion.69 = f32[512,512]{1,0:T(8,128)S(1)} fusion(f32[512,512]{1,0:T(8,128)S(1)} %fusion.15), kind=kOutput, calls=%fused_computation.88 | convolution fusion | flops 1610612736 | bytes 2097152 | tf_op jit(solution)/shard_map/dot_general | solution.py:17
  40.9 1.9 %fusion.9 = f32[512,512]{1,0:T(8,128)S(1)} fusion(f32[512,512]{1,0:T(8,128)S(1)} %fusion.69, f32[]{:T(128)S(6)} %div.14, f32[256,512]{1,0:T(8,128)S(1)} %broadcast_select_fusion, f32[256,512]{1,0:T(8,128)S(1)} %convert_element_type.20, pred[]{:T(512)S(6)} %eq.23), kind=kOutput, calls=%fused_computation.20 | convolution fusion | flops 1612447744 | bytes 3145733 | tf_op jit(solution)/shard_map/dot_general | solution.py:17
  42.8 1.9 %fusion.11 = f32[512,512]{1,0:T(8,128)S(1)} fusion(f32[512,512]{1,0:T(8,128)S(1)} %fusion.9), kind=kOutput, calls=%fused_computation.22 | convolution fusion | flops 1611661312 | bytes 2097152 | tf_op jit(solution)/shard_map/dot_general | solution.py:17
  44.8 1.9 %fusion.13 = f32[512,512]{1,0:T(8,128)S(1)} fusion(f32[512,512]{1,0:T(8,128)S(1)} %fusion.7, f32[512,512]{1,0:T(8,128)S(1)} %fusion.9), kind=kOutput, calls=%fused_computation.23 | convolution fusion | flops 1611661312 | bytes 3145728 | tf_op jit(solution)/shard_map/dot_general | solution.py:17
  46.7 2.0 %fusion.70 = f32[512,512]{1,0:T(8,128)S(1)} fusion(f32[512,512]{1,0:T(8,128)S(1)} %fusion.11), kind=kOutput, calls=%fused_computation.89 | convolution fusion | flops 1610612736 | bytes 2097152 | tf_op jit(solution)/shard_map/dot_general | solution.py:17
  48.7 1.9 %fusion = f32[512,512]{1,0:T(8,128)S(1)} fusion(f32[512,512]{1,0:T(8,128)S(1)} %fusion.70, f32[512,512]{1,0:T(8,128)S(1)} %fusion.9), kind=kOutput, calls=%fused_computation.3 | convolution fusion | flops 1611661312 | bytes 3145728 | tf_op jit(solution)/shard_map/dot_general | solution.py:17
  50.6 1.9 %convolution_convert_fusion = bf16[512,512]{1,0:T(8,128)(2,1)S(1)} fusion(f32[512,512]{1,0:T(8,128)S(1)} %fusion.13, f32[512,512]{1,0:T(8,128)S(1)} %fusion), kind=kOutput, calls=%fused_computation.4 | convolution fusion | flops 1610874880 | bytes 2621440 | tf_op jit(solution)/shard_map/dot_general | solution.py:17
  52.5 0.4 collective-permute-start.3
  53.6 0.0 all-to-all-done.1
  53.6 0.0 copy-start.4
  53.6 0.0 copy-start.6
  53.6 0.7 %copy.15 = bf16[8,8,8,256]{3,2,0,1:T(8,128)(2,1)} copy(bf16[8,8,8,256]{3,2,1,0:T(8,128)(2,1)S(1)} %bitcast.83) | data formatting | bytes 524288 | tf_op jit(solution)/shard_map/reshape | solution.py:82
  54.3 0.0 collective-permute-done.3
  54.3 0.3 copy-done.4
  54.6 0.1 copy-done.6
  54.7 0.9 %fusion.42 = (bf16[1,256,512]{2,1,0:T(8,128)(2,1)}, bf16[1,256,512]{2,1,0:T(8,128)(2,1)}) fusion(bf16[1,256,512]{2,1,0:T(8,128)(2,1)S(1)} %copy-done.6, bf16[256,512]{1,0:T(8,128)(2,1)S(1)} %collective-permute-done.3, pred[]{:T(512)S(6)} %eq.23, pred[]{:T(512)} %bitcast.21, bf16[512,512]{1,0:T(8,128)(2,1)S(1)} %convolution_convert_fusion, s32[]{:T(128)S(6)} %select_n.72, ...), kind=kLoop, calls=%fused_computation.53 | loop fusion | flops 524288 | bytes 1572870 | tf_op jit(solution)/shard_map/broadcast_in_dim | solution.py:107
  (8 shorter events, 0.1 us)
Async XLA Ops:
  2.3 6.5 %copy-start.3 = (bf16[1,256,512]{2,1,0:T(8,128)(2,1)S(1)}, bf16[1,256,512]{2,1,0:T(8,128)(2,1)}, u32[]{:S(2)}) copy-start(bf16[1,256,512]{2,1,0:T(8,128)(2,1)} %param.9) | copy-start | bytes 786436
  2.3 17.7 %copy-start.5 = (bf16[1,256,512]{2,1,0:T(8,128)(2,1)S(1)}, bf16[1,256,512]{2,1,0:T(8,128)(2,1)}, u32[]{:S(2)}) copy-start(bf16[1,256,512]{2,1,0:T(8,128)(2,1)} %param.10) | copy-start | bytes 786436
  2.3 16.2 %all-to-all-start = ((bf16[64,8,256]{2,0,1:T(8,128)(2,1)}), bf16[64,8,256]{2,0,1:T(8,128)(2,1)S(1)}, u32[]{:S(2)}, u32[]{:S(2)}) async-start(bf16[64,8,256]{2,0,1:T(8,128)(2,1)} %bitcast.79), calls=%async_computation | async-start | bytes 524288 | tf_op jit(solution)/shard_map/all_to_all | solution.py:54
  8.8 9.7 %collective-permute-start = (bf16[256,512]{1,0:T(8,128)(2,1)S(1)}, bf16[256,512]{1,0:T(8,128)(2,1)S(1)}, u32[]{:S(2)}, u32[]{:S(2)}) collective-permute-start(bf16[256,512]{1,0:T(8,128)(2,1)S(1)} %bitcast.88), channel_id=1, source_target_pairs={{0,1},{1,0},{2,3},{3,2},{4,5},{5,4},{6,7},{7,6},{8,9},{9,8},{10,11... | collective-permute-start | bytes 786440 | tf_op jit(solution)/shard_map/ppermute | solution.py:13
  18.5 1.5 %collective-permute-start.1 = (bf16[512,256]{1,0:T(8,128)(2,1)S(1)}, bf16[512,256]{1,0:T(8,128)(2,1)S(1)}, u32[]{:S(2)}, u32[]{:S(2)}) collective-permute-start(bf16[512,256]{1,0:T(8,128)(2,1)S(1)} %bitcast.84), channel_id=1, source_target_pairs={{0,1},{1,0},{2,3},{3,2},{4,5},{5,4},{6,7},{7,6},{8,9},{9,8},{10,11... | collective-permute-start | bytes 786440 | tf_op jit(solution)/shard_map/ppermute | solution.py:13
  25.8 27.8 %all-to-all-start.1 = ((bf16[8,64,256]{2,1,0:T(8,128)(2,1)}), bf16[8,64,256]{2,1,0:T(8,128)(2,1)S(1)}, u32[]{:S(2)}, u32[]{:S(2)}) async-start(bf16[8,64,256]{2,1,0:T(8,128)(2,1)} %fusion.44), calls=%async_computation.1 | async-start | bytes 524288 | tf_op jit(solution)/shard_map/all_to_all | solution.py:83
  29.2 1.0 %copy-start.7 = (f32[1,256,512]{2,1,0:T(8,128)S(1)}, f32[1,256,512]{2,1,0:T(8,128)}, u32[]{:S(2)}) copy-start(f32[1,256,512]{2,1,0:T(8,128)} %param.8) | copy-start | bytes 1572868
  30.2 1.0 %copy-start.2 = (f32[1,256,512]{2,1,0:T(8,128)S(1)}, f32[1,256,512]{2,1,0:T(8,128)}, u32[]{:S(2)}) copy-start(f32[1,256,512]{2,1,0:T(8,128)} %param.7) | copy-start | bytes 1572868
  31.3 0.9 %copy-start = (f32[256,512]{1,0:T(8,128)}, f32[256,512]{1,0:T(8,128)S(1)}, u32[]{:S(2)}) copy-start(f32[256,512]{1,0:T(8,128)S(1)} %fusion.2) | copy-start | bytes 1572868
  31.6 0.8 %copy-start.1 = (f32[256,512]{1,0:T(8,128)}, f32[256,512]{1,0:T(8,128)S(1)}, u32[]{:S(2)}) copy-start(f32[256,512]{1,0:T(8,128)S(1)} %get-tuple-element.8) | copy-start | bytes 1572868
  31.6 1.6 %collective-permute-start.2 = (bf16[256,512]{1,0:T(8,128)(2,1)S(1)}, bf16[256,512]{1,0:T(8,128)(2,1)S(1)}, u32[]{:S(2)}, u32[]{:S(2)}) collective-permute-start(bf16[256,512]{1,0:T(8,128)(2,1)S(1)} %get-tuple-element.7), channel_id=1, source_target_pairs={{0,1},{1,0},{2,3},{3,2},{4,5},{5,4},{6,7},{7,6},{8,9},{9,8},{10,11... | collective-permute-start | bytes 786440 | tf_op jit(solution)/shard_map/ppermute | solution.py:13
  52.5 1.8 %collective-permute-start.3 = (bf16[256,512]{1,0:T(8,128)(2,1)S(1)}, bf16[256,512]{1,0:T(8,128)(2,1)S(1)}, u32[]{:S(2)}, u32[]{:S(2)}) collective-permute-start(bf16[256,512]{1,0:T(8,128)(2,1)S(1)} %constant_dynamic-slice_fusion), channel_id=1, source_target_pairs={{0,1},{1,0},{2,3},{3,2},{4,5},{5,4},{6,7},{7,6},{8,9},{9,8},{10,11... | collective-permute-start | bytes 786440 | tf_op jit(solution)/shard_map/ppermute | solution.py:13
  53.6 1.0 %copy-start.4 = (bf16[1,256,512]{2,1,0:T(8,128)(2,1)S(1)}, bf16[1,256,512]{2,1,0:T(8,128)(2,1)}, u32[]{:S(2)}) copy-start(bf16[1,256,512]{2,1,0:T(8,128)(2,1)} %param.9) | copy-start | bytes 786436
  53.6 1.1 %copy-start.6 = (bf16[1,256,512]{2,1,0:T(8,128)(2,1)S(1)}, bf16[1,256,512]{2,1,0:T(8,128)(2,1)}, u32[]{:S(2)}) copy-start(bf16[1,256,512]{2,1,0:T(8,128)(2,1)} %param.10) | copy-start | bytes 786436
